TPU v7x, 256 devices: a whole 4x4x8 slice. The times are simulated.
256 devices in a mesh: enc: 8 (over z), kr: 8 (over x_lo, y), kc: 4 (over x_hi, core).
Axes of the slice: x: 4 (x_hi: 2, x_lo: 2; x = x_hi * 2 + x_lo), y: 4, z: 8, core: 2. Of those that a mesh axis runs over, the one named last changes fastest.
Arguments:
- inputs: bfloat16 [49152, 1024], P(('enc', 'kr', 'kc')), may hold values from -24 to 24
- w_first: bfloat16 [1024, 1024], replicated, may hold values from -0.1875 to 0.1875
- w_second: bfloat16 [1024, 64], replicated, may hold values from -0.1875 to 0.1875
- inv_length: float32 [64], replicated, may hold values from 0.05 to 1.8
- probes: bfloat16 [49152, 128], P(('enc', 'kr', 'kc')), may hold values from -6 to 6
- solves: bfloat16 [49152, 128], P(('enc', 'kr', 'kc')), may hold values from -6 to 6
Outputs:
- products: bfloat16 [49152, 128], P(('enc', 'kr', 'kc'))
- grad_first: float32 [1024, 1024], P(('enc', 'kr', 'kc'))
- grad_second: float32 [1024, 64], P(('enc', 'kr', 'kc'))
All inputs are finite; a program needn't handle non-finite values.
Results may differ from a plain program's by a relative error of at most 0.007.
The roundings to bfloat16 on the way count: a program that leaves them out, or rounds other values in their place, can miss the bound.
Values may be sent and summed in bfloat16 or wider, within the bound.
A program may use at most 64 MiB of HBM per device.

v0:
```python
import math
import jax
import jax.numpy as jnp
from jax import lax
from jax.sharding import PartitionSpec as P

probe_gain = 0.5
loss_gain = 0.02


def contract_inner(left, right):
    return lax.dot_general(
        left, right, (((1,), (1,)), ((), ())), preferred_element_type=jnp.float32
    )


def contract_outer(left, right):
    return lax.dot_general(
        left, right, (((0,), (0,)), ((), ())), preferred_element_type=jnp.float32
    )


def kernel_tile(row_feat, row_norm, col_feat):
    col_wide = col_feat.astype(jnp.float32)
    col_norm = jnp.sum(col_wide * col_wide, axis=1)
    cross = contract_inner(row_feat, col_feat)
    return jnp.exp(-0.5 * (row_norm[:, None] + col_norm[None, :] - 2.0 * cross))


def split_blocks(array):
    length = array.shape[0]
    candidates = [
        option_width
        for option_width in (1024, 768, 512, 384, 256, 192, 128)
        if length % option_width == 0
    ]
    width = candidates[0]
    return array.reshape(length // width, width, array.shape[1])


def row_totals(parts):
    return (
        lax.psum_scatter(parts[0], "kc", scatter_dimension=0, tiled=True),
        lax.psum_scatter(parts[1], "kc", scatter_dimension=0, tiled=True),
        lax.psum_scatter(parts[2], "kc", scatter_dimension=0, tiled=True),
    )


def local(inputs, w_first, w_second, inv_length, probes, solves):
    pre = jnp.dot(inputs, w_first, preferred_element_type=jnp.float32)
    hidden = jax.nn.silu(pre).astype(jnp.bfloat16)
    features = jnp.dot(hidden, w_second, preferred_element_type=jnp.float32)
    scaled = (features * inv_length[None, :]).astype(jnp.bfloat16)
    own_wide = scaled.astype(jnp.float32)
    own_rows = inputs.shape[0]
    row_count = own_rows * lax.axis_size("kc")
    feat_width = scaled.shape[1]
    probe_width = probes.shape[1]
    zeros_init = (
        jnp.zeros((row_count, probe_width), jnp.float32),
        jnp.zeros((row_count, feat_width), jnp.float32),
        jnp.zeros((row_count,), jnp.float32),
    )
    row_feat, row_probe, row_solve = (
        lax.all_gather(scaled, "kc", axis=0, tiled=True),
        lax.all_gather(probes, "kc", axis=0, tiled=True),
        lax.all_gather(solves, "kc", axis=0, tiled=True),
    )
    row_wide = row_feat.astype(jnp.float32)
    row_norm = jnp.sum(row_wide * row_wide, axis=1)
    portion = (
        lax.all_gather(scaled, ("enc", "kr"), axis=0, tiled=True),
        lax.all_gather(probes, ("enc", "kr"), axis=0, tiled=True),
        lax.all_gather(solves, ("enc", "kr"), axis=0, tiled=True),
    )

    def advance(totals, columns):
        col_feat, col_probe, col_solve = columns
        kernel = kernel_tile(row_feat, row_norm, col_feat)
        first = kernel * contract_inner(row_solve, col_probe)
        second = kernel * contract_inner(row_probe, col_solve)
        mixed_part = jnp.dot(
            first.astype(jnp.bfloat16), col_feat, preferred_element_type=jnp.float32
        ) + jnp.dot(second.astype(jnp.bfloat16), col_feat, preferred_element_type=jnp.float32)
        vpart = jnp.dot(kernel.astype(jnp.bfloat16), col_probe, preferred_element_type=jnp.float32)
        return (
            (
                totals[0] + vpart,
                totals[1] + mixed_part,
                totals[2] + jnp.sum(first, axis=1) + jnp.sum(second, axis=1),
            ),
            None,
        )

    stacked = tuple((split_blocks(item) for item in portion))
    result, _ = lax.scan(advance, zeros_init, stacked)
    vsum, mixed, sums = row_totals(result)
    products = (vsum * probe_gain).astype(jnp.bfloat16)
    lscale = loss_gain / math.sqrt(probe_width)
    dfeat = -lscale * inv_length[None, :] * (sums[:, None] * own_wide - mixed)
    dfeat_half = dfeat.astype(jnp.bfloat16)
    second_term = contract_outer(hidden, dfeat_half)
    back_hidden = contract_inner(dfeat_half, w_second)
    sigma = jax.nn.sigmoid(pre)
    dpre = (back_hidden * sigma * (1.0 + pre * (1.0 - sigma))).astype(jnp.bfloat16)
    first_term = contract_outer(inputs, dpre)
    grad_first, grad_second = (
        lax.psum_scatter(first_term, ("enc", "kr", "kc"), scatter_dimension=0, tiled=True),
        lax.psum_scatter(second_term, ("enc", "kr", "kc"), scatter_dimension=0, tiled=True),
    )
    return (products, grad_first, grad_second)


def solution(mesh):
    in_specs = (
        P(("enc", "kr", "kc"), None),
        P(),
        P(),
        P(),
        P(("enc", "kr", "kc"), None),
        P(("enc", "kr", "kc"), None),
    )
    out_specs = (
        P(("enc", "kr", "kc"), None),
        P(("enc", "kr", "kc"), None),
        P(("enc", "kr", "kc"), None),
    )
    return jax.shard_map(local, mesh=mesh, in_specs=in_specs, out_specs=out_specs, check_vma=False)
```

profile of v0, /device:TPU:97, one launch (start us, length us, event | category | flops | bytes accessed | tf_op | source)
XLA Modules:
  0.0 1431.5 jit_solution(13192146417634224073)
XLA Ops:
  7.2 1.5 copy-done
  8.8 2.5 multiply_convert_fusion
  13.8 7.6 all-gather
  23.1 7.3 all_gather.21
  30.4 7.4 all_gather.23
  38.7 217.8 %all-gather.10.cloned.1.call-done = bf16[64,192,64]{1,2,0:T(8,128)(2,1)} async-done(((bf16[1,192,64]{1,2,0:T(8,128)(2,1)}), bf16[64,192,64]{1,2,0:T(8,128)(2,1)}) %all-gather.10.cloned.1.call-update) | async-done | bytes 1572880 | tf_op jit(solution)/shard_map/all_gather | solution.py:72
  256.5 4.6 copy.20
  261.1 295.6 %all-gather.6.cloned.1.call-done = bf16[12288,128]{1,0:T(8,128)(2,1)} async-done(((bf16[192,128]{1,0:T(8,128)(2,1)}), bf16[12288,128]{1,0:T(8,128)(2,1)}) %all-gather.6.cloned.1.call-update) | async-done | bytes 3145744 | tf_op jit(solution)/shard_map/all_gather | solution.py:73
  556.7 300.3 %all-gather.8.cloned.1.call-done = bf16[12288,128]{1,0:T(8,128)(2,1)} async-done(((bf16[192,128]{1,0:T(8,128)(2,1)}), bf16[12288,128]{1,0:T(8,128)(2,1)}) %all-gather.8.cloned.1.call-update) | async-done | bytes 3145744 | tf_op jit(solution)/shard_map/all_gather | solution.py:74
  857.0 162.3 %while.15 = (s32[]{:T(128)}, f32[768,128]{1,0:T(8,128)S(1)}, f32[768,64]{0,1:T(8,128)S(1)}, f32[768]{0:T(1024)S(1)}, f32[768]{0:T(1024)S(1)}, /*index=5*/bf16[12...) while((s32[]{:T(128)}, f32[768,128]{1,0:T(8,128)S(1)}, ...), condition=%wide.region_5.6_spmd.clone, body=%wide.region_1.5_spmd.clone.sunk | while | flops 915160832 | bytes 35353800 | solution.py:96
  858.2 3.5 fusion.88
  861.6 2.7 fusion.89
  864.5 1.5 fusion.90
  867.5 1.5 fusion.92
  871.7 3.5 fusion.88
  875.2 2.7 fusion.89
  878.1 1.5 fusion.90
  881.0 1.5 fusion.92
  885.2 3.5 fusion.88
  888.7 2.7 fusion.89
  891.6 1.5 fusion.90
  894.5 1.5 fusion.92
  898.7 3.5 fusion.88
  902.2 2.7 fusion.89
  905.1 1.5 fusion.90
  908.1 1.5 fusion.92
  912.3 3.5 fusion.88
  915.7 2.7 fusion.89
  918.6 1.5 fusion.90
  921.6 1.5 fusion.92
  925.8 3.5 fusion.88
  929.2 2.7 fusion.89
  932.2 1.5 fusion.90
  935.1 1.5 fusion.92
  939.3 3.5 fusion.88
  942.8 2.7 fusion.89
  945.7 1.5 fusion.90
  948.6 1.5 fusion.92
  952.8 3.5 fusion.88
  956.3 2.7 fusion.89
  959.2 1.5 fusion.90
  962.2 1.5 fusion.92
  966.3 3.5 fusion.88
  969.8 2.7 fusion.89
  972.7 1.5 fusion.90
  975.7 1.5 fusion.92
  979.9 3.5 fusion.88
  983.3 2.7 fusion.89
  986.3 1.5 fusion.90
  989.2 1.5 fusion.92
  993.4 3.5 fusion.88
  996.9 2.7 fusion.89
  999.8 1.5 fusion.90
  1002.7 1.5 fusion.92
  1006.9 3.5 fusion.88
  1010.4 2.7 fusion.89
  1013.3 1.5 fusion.90
  1016.2 1.5 fusion.92
  1021.5 53.3 %all-reduce = f32[768]{0:T(1024)S(1)} all-reduce(f32[768]{0:T(1024)S(1)} %get-tuple-element.63), channel_id=3, replica_groups=mesh['enc'=8,'kr'=8,'kc'=4] {'kc'}, use_global_device_ids=true, to_apply=%region_7.8.clone | all-reduce | flops 768 | bytes 6144
  1075.0 33.0 %reduce-scatter.8.cloned.1.call-done = f32[192,64]{1,0:T(8,128)} async-done(((f32[768,64]{1,0:T(8,128)}), f32[192,64]{1,0:T(8,128)}) %reduce-scatter.8.cloned.1.call-update) | async-done | bytes 49168
  1110.3 4.2 convolution_bitcast_fusion
  1114.6 28.4 %reduce-scatter.6.cloned.1.call-done = f32[192,128]{1,0:T(8,128)} async-done(((f32[768,128]{1,0:T(8,128)}), f32[192,128]{1,0:T(8,128)}) %reduce-scatter.6.cloned.1.call-update) | async-done | bytes 98320 | tf_op jit(solution)/shard_map/reduce_scatter | solution.py:43
  1143.0 1.5 multiply_convert_fusion.1
  1144.5 276.8 %all-reduce.6.cloned.1.call-done = (f32[1024,1024]{0,1:T(8,128)}, f32[1024,64]{1,0:T(8,128)}) async-done(((f32[1024,1024]{0,1:T(8,128)}, f32[1024,64]{1,0:T(8,128)}), (f32[1024,1024]{0,1:T(8,128)}, f32[1024,64]{1,0:T(8,128)})) %all-reduce.6.cloned.1.call-update) | async-done | bytes 4456464
  (117 shorter events, 62.3 us)
Async XLA Ops:
  7.2 1.6 copy-start
  7.2 4.1 copy-start.6
  7.2 4.1 copy-start.7
  7.2 249.3 %all-gather.10.cloned.1.call-start = ((), (), s32[]{:S(2)}) async-start(), calls=%async_computation.5 | async-start | bytes 2129920 | tf_op jit(solution)/shard_map/all_gather | solution.py:72
  8.8 21.6 %copy-start.5 = (bf16[192,128]{1,0:T(8,128)(2,1)S(1)}, bf16[192,128]{1,0:T(8,128)(2,1)}, u32[]{:S(2)}) copy-start(bf16[192,128]{1,0:T(8,128)(2,1)} %param.12) | copy-start | bytes 147460
  12.2 544.5 %all-gather.6.cloned.1.call-start = ((), (), s32[]{:S(2)}) async-start(), calls=%async_computation.2 | async-start | bytes 3194880 | tf_op jit(solution)/shard_map/all_gather | solution.py:73
  13.0 844.0 %all-gather.8.cloned.1.call-start = ((), (), s32[]{:S(2)}) async-start(), calls=%async_computation.3 | async-start | bytes 3194880 | tf_op jit(solution)/shard_map/all_gather | solution.py:74
  13.7 1094.4 %reduce-scatter.8.cloned.1.call-start = ((), (), s32[]{:S(2)}) async-start(), calls=%async_computation.6 | async-start | bytes 491520
  21.7 0.6 copy-start.3
  857.0 163.3 %copy-start.8 = (u32[256]{0:T(256)S(1)}, u32[256]{0:T(256)}, u32[]{:S(2)}) copy-start(u32[256]{0:T(256)} %constant.36) | copy-start | bytes 3076
  857.0 252.1 %copy-start.4 = (bf16[192,64]{0,1:T(8,128)(2,1)S(1)}, bf16[192,64]{0,1:T(8,128)(2,1)}, u32[]{:S(2)}) copy-start(bf16[192,64]{0,1:T(8,128)(2,1)} %fusion.38) | copy-start | bytes 73732
  861.6 2.9 copy-start.1
  875.2 2.9 copy-start.1
  888.7 2.9 copy-start.1
  902.2 2.9 copy-start.1
  915.7 2.9 copy-start.1
  929.2 2.9 copy-start.1
  942.8 2.9 copy-start.1
  956.3 2.9 copy-start.1
  969.8 2.9 copy-start.1
  983.3 2.9 copy-start.1
  996.9 2.9 copy-start.1
  1010.4 2.9 copy-start.1
  1019.3 55.6 %copy-start.2 = (f32[768,128]{1,0:T(8,128)}, f32[768,128]{1,0:T(8,128)S(1)}, u32[]{:S(2)}) copy-start(f32[768,128]{1,0:T(8,128)S(1)} %get-tuple-element.62) | copy-start | bytes 1179652
  1020.2 122.8 %reduce-scatter.6.cloned.1.call-start = ((), (), s32[]{:S(2)}) async-start(), calls=%async_computation.4 | async-start | bytes 491520 | tf_op jit(solution)/shard_map/reduce_scatter | solution.py:43
  1074.9 346.5 %all-reduce.6.cloned.1.call-start = ((), (), s32[]{:S(2)}) async-start(), calls=%async_computation.7 | async-start | bytes 9437184
Sparse Core Ops, SparseCore 0:
  12.3 244.0 all-gather.9
  258.3 298.3 all-gather.5
  558.5 298.4 all-gather.7
  1020.3 87.6 reduce-scatter.7
  1110.7 32.2 reduce-scatter.5
  1148.4 272.9 all-reduce.5
where the time goes:
time: 1430 us
  waiting for transfers between devices  1150 us (80%)
  matrix products  154 us (11%)
  blocking collectives  75.6 us (5%)
  other arithmetic  16.6 us (1%)
  local copies, waits for them, and re-layouts  15.8 us (1%)
  between operations  14.9 us (1%)
    unnamed x8, waiting for transfers between devices  311 us
    all_gather x1, waiting for transfers between devices, local(): lax.all_gather(solves, ('enc', 'kr'), axis=0, tiled=True)  300 us
    all_gather x1, waiting for transfers between devices, local(): lax.all_gather(probes, ('enc', 'kr'), axis=0, tiled=True)  296 us
    all_gather x1, waiting for transfers between devices, local(): lax.all_gather(scaled, ('enc', 'kr'), axis=0, tiled=True)  218 us
    dot_general x36, matrix products, contract_inner(): lax.dot_general(left, right, (((1,), (1,)), ((), ())), preferred_element_...  78.7 us
    unnamed x1, blocking collectives  53.3 us
    dot_general x12, matrix products, advance(): jnp.dot(kernel.astype(jnp.bfloat16), col_probe, preferred_element_type=jn...  32.7 us
  transfers between devices with their start and end apart: 6, of which 6 were waited for; matrix products, arithmetic and copies ran while one was open for 1% of the time, Pallas kernels for 0%

commit v1 on v0

--- a/solution.py
+++ b/solution.py
@@ -6,6 +6,11 @@
 
 probe_gain = 0.5
 loss_gain = 0.02
+
+
+def all_by_exchange(shard, name, d):
+    stack = jnp.stack([shard] * lax.axis_size(name))
+    return jnp.concatenate(lax.all_to_all(stack, name, 0, 0), axis=d)
 
 
 def contract_inner(left, right):
@@ -70,7 +75,7 @@
     row_norm = jnp.sum(row_wide * row_wide, axis=1)
     portion = (
         lax.all_gather(scaled, ("enc", "kr"), axis=0, tiled=True),
-        lax.all_gather(probes, ("enc", "kr"), axis=0, tiled=True),
+        all_by_exchange(probes, ("enc", "kr"), 0),
         lax.all_gather(solves, ("enc", "kr"), axis=0, tiled=True),
     )
 

time: 1430 us -> 1150 us (0.80)
  waiting for transfers between devices: 1150 us -> 837 us
    all_gather x1 -> x0, waiting for transfers between devices: 296 us -> none  [local(): lax.all_gather(probes, ('enc', 'kr'), axis=0, tiled=True)]
    unnamed x8 -> x7, waiting for transfers between devices: 311 us -> 311 us
  transfers between devices with their start and end apart: 6 -> 6, of which waited for: 6 -> 5; matrix products, arithmetic and copies ran while one was open for 1% -> 2% of each run, Pallas kernels for 0% -> 0%
where the time goes in v1:
time: 1150 us; the launch traced here: 1140 us
  waiting for transfers between devices  837 us (73%)
  matrix products  154 us (13%)
  blocking collectives  84.6 us (7%)
  local copies, waits for them, and re-layouts  25.3 us (2%)
  other arithmetic  16.5 us (1%)
  between operations  14.6 us (1%)
  starting transfers between devices  11.8 us (1%)
    unnamed x7, waiting for transfers between devices  311 us
    all_gather x1, waiting for transfers between devices, local(): lax.all_gather(solves, ('enc', 'kr'), axis=0, tiled=True)  291 us
    all_gather x1, waiting for transfers between devices, local(): lax.all_gather(scaled, ('enc', 'kr'), axis=0, tiled=True)  206 us
    dot_general x36, matrix products, contract_inner(): lax.dot_general(left, right, (((1,), (1,)), ((), ())), preferred_element_...  78.6 us
    unnamed x1, blocking collectives  53.4 us
    dot_general x12, matrix products, advance(): jnp.dot(kernel.astype(jnp.bfloat16), col_probe, preferred_element_type=jn...  32.7 us
    reduce_scatter x1, waiting for transfers between devices, row_totals(): lax.psum_scatter(parts[0], 'kc', scatter_dimension=0, tiled=True)  28.4 us
  transfers between devices with their start and end apart: 6, of which 5 were waited for; matrix products, arithmetic and copies ran while one was open for 2% of the time, Pallas kernels for 0%

profile of v1, /device:TPU:97, one launch (start us, length us, event | category | flops | bytes accessed | tf_op | source)
XLA Modules:
  0.0 1144.5 jit_solution(8856312092959807326)
XLA Ops:
  8.8 2.5 multiply_convert_fusion
  12.2 2.4 stack.2
  14.6 11.6 %all-to-all-start = ((bf16[64,192,128]{2,1,0:T(8,128)(2,1)}), bf16[64,192,128]{2,1,0:T(8,128)(2,1)}, u32[]{:S(2)}, u32[]{:S(2)}) async-start(bf16[64,192,128]{2,1,0:T(8,128)(2,1)} %stack.2), calls=%async_computation | async-start | bytes 6291456 | tf_op jit(solution)/shard_map/all_to_all | solution.py:13
  27.0 12.8 %all-gather = bf16[4,192,64]{1,2,0:T(8,128)(2,1)S(1)} all-gather(bf16[1,192,64]{1,2,0:T(8,128)(2,1)S(1)} %bitcast.85), channel_id=1, replica_groups=mesh['enc'=8,'kr'=8,'kc'=4] {'kc'}, dimensions={0}, use_global_device_ids=true | all-gather | bytes 122880 | tf_op jit(solution)/shard_map/all_gather | solution.py:70
  41.5 8.7 all_gather.17
  50.3 9.5 all_gather.19
  60.7 206.3 %all-gather.7.cloned.1.call-done = bf16[64,192,64]{1,2,0:T(8,128)(2,1)} async-done(((bf16[1,192,64]{1,2,0:T(8,128)(2,1)}), bf16[64,192,64]{1,2,0:T(8,128)(2,1)}) %all-gather.7.cloned.1.call-update) | async-done | bytes 1572880 | tf_op jit(solution)/shard_map/all_gather | solution.py:77
  267.1 4.6 copy.20
  271.6 291.4 %all-gather.5.cloned.1.call-done = bf16[12288,128]{1,0:T(8,128)(2,1)} async-done(((bf16[192,128]{1,0:T(8,128)(2,1)}), bf16[12288,128]{1,0:T(8,128)(2,1)}) %all-gather.5.cloned.1.call-update) | async-done | bytes 3145744 | tf_op jit(solution)/shard_map/all_gather | solution.py:79
  563.1 169.4 %while.15 = (s32[]{:T(128)}, f32[768,128]{1,0:T(8,128)S(1)}, f32[768,64]{0,1:T(8,128)S(1)}, f32[768]{0:T(1024)}, f32[768]{0:T(1024)S(1)}, /*index=5*/bf16[12,102...) while((s32[]{:T(128)}, f32[768,128]{1,0:T(8,128)S(1)}, ...), condition=%wide.region_5.6_spmd.clone, body=%wide.region_1.5_spmd.clone.sunk | while | flops 915160832 | bytes 35378432 | solution.py:101
  564.2 3.5 fusion.88
  567.7 2.7 fusion.89
  570.6 1.5 fusion.90
  573.6 1.6 fusion.92
  578.4 3.5 fusion.88
  581.8 2.7 fusion.89
  584.7 1.5 fusion.90
  587.7 1.6 fusion.92
  592.5 3.5 fusion.88
  595.9 2.7 fusion.89
  598.8 1.5 fusion.90
  601.8 1.6 fusion.92
  606.6 3.5 fusion.88
  610.0 2.7 fusion.89
  613.0 1.5 fusion.90
  615.9 1.6 fusion.92
  620.7 3.5 fusion.88
  624.2 2.7 fusion.89
  627.1 1.5 fusion.90
  630.0 1.6 fusion.92
  634.8 3.5 fusion.88
  638.3 2.7 fusion.89
  641.2 1.5 fusion.90
  644.1 1.6 fusion.92
  648.9 3.5 fusion.88
  652.4 2.7 fusion.89
  655.3 1.5 fusion.90
  658.3 1.6 fusion.92
  663.0 3.5 fusion.88
  666.5 2.7 fusion.89
  669.4 1.5 fusion.90
  672.4 1.6 fusion.92
  677.2 3.5 fusion.88
  680.6 2.7 fusion.89
  683.5 1.5 fusion.90
  686.5 1.6 fusion.92
  691.3 3.5 fusion.88
  694.7 2.7 fusion.89
  697.6 1.5 fusion.90
  700.6 1.6 fusion.92
  705.4 3.5 fusion.88
  708.8 2.7 fusion.89
  711.8 1.5 fusion.90
  714.7 1.6 fusion.92
  719.5 3.5 fusion.88
  723.0 2.7 fusion.89
  725.9 1.5 fusion.90
  728.8 1.6 fusion.92
  734.7 53.4 %all-reduce = f32[768]{0:T(1024)S(1)} all-reduce(f32[768]{0:T(1024)} %get-tuple-element.63), channel_id=3, replica_groups=mesh['enc'=8,'kr'=8,'kc'=4] {'kc'}, use_global_device_ids=true, to_apply=%region_7.8.clone | all-reduce | flops 768 | bytes 6144
  788.3 32.9 %reduce-scatter.8.cloned.1.call-done = f32[192,64]{1,0:T(8,128)} async-done(((f32[768,64]{1,0:T(8,128)}), f32[192,64]{1,0:T(8,128)}) %reduce-scatter.8.cloned.1.call-update) | async-done | bytes 49168
  823.4 4.3 convolution_bitcast_fusion
  827.7 28.4 %reduce-scatter.6.cloned.1.call-done = f32[192,128]{1,0:T(8,128)} async-done(((f32[768,128]{1,0:T(8,128)}), f32[192,128]{1,0:T(8,128)}) %reduce-scatter.6.cloned.1.call-update) | async-done | bytes 98320 | tf_op jit(solution)/shard_map/reduce_scatter | solution.py:48
  856.1 1.5 multiply_convert_fusion.1
  857.6 277.0 %all-reduce.6.cloned.1.call-done = (f32[1024,1024]{0,1:T(8,128)}, f32[1024,64]{1,0:T(8,128)}) async-done(((f32[1024,1024]{0,1:T(8,128)}, f32[1024,64]{1,0:T(8,128)}), (f32[1024,1024]{0,1:T(8,128)}, f32[1024,64]{1,0:T(8,128)})) %all-reduce.6.cloned.1.call-update) | async-done | bytes 4456464
  (169 shorter events, 70.2 us)
Async XLA Ops:
  7.2 1.6 copy-start
  7.2 4.1 copy-start.9
  7.2 4.1 copy-start.10
  7.2 259.8 %all-gather.7.cloned.1.call-start = ((), (), s32[]{:S(2)}) async-start(), calls=%async_computation.5 | async-start | bytes 2129920 | tf_op jit(solution)/shard_map/all_gather | solution.py:77
  8.8 3.4 copy-start.6
  14.6 12.4 %copy-start.4 = (bf16[192,64]{0,1:T(8,128)(2,1)S(1)}, bf16[192,64]{0,1:T(8,128)(2,1)}, u32[]{:S(2)}) copy-start(bf16[192,64]{0,1:T(8,128)(2,1)} %fusion.38) | copy-start | bytes 73732
  14.6 26.9 %copy-start.5 = (bf16[192,128]{1,0:T(8,128)(2,1)S(1)}, bf16[192,128]{1,0:T(8,128)(2,1)}, u32[]{:S(2)}) copy-start(bf16[192,128]{1,0:T(8,128)(2,1)} %param.13) | copy-start | bytes 147460
  14.6 257.1 %all-to-all-start = ((bf16[64,192,128]{2,1,0:T(8,128)(2,1)}), bf16[64,192,128]{2,1,0:T(8,128)(2,1)}, u32[]{:S(2)}, u32[]{:S(2)}) async-start(bf16[64,192,128]{2,1,0:T(8,128)(2,1)} %stack.2), calls=%async_computation | async-start | bytes 6291456 | tf_op jit(solution)/shard_map/all_to_all | solution.py:13
  26.1 536.9 %all-gather.5.cloned.1.call-start = ((), (), s32[]{:S(2)}) async-start(), calls=%async_computation.3 | async-start | bytes 3194880 | tf_op jit(solution)/shard_map/all_gather | solution.py:79
  26.9 794.3 %reduce-scatter.8.cloned.1.call-start = ((), (), s32[]{:S(2)}) async-start(), calls=%async_computation.6 | async-start | bytes 491520
  40.1 0.6 copy-start.3
  563.0 170.4 %copy-start.12 = (u32[256]{0:T(256)S(1)}, u32[256]{0:T(256)}, u32[]{:S(2)}) copy-start(u32[256]{0:T(256)} %constant.36) | copy-start | bytes 3076
  563.1 171.6 %copy-start.11 = (f32[64]{0:T(128)S(1)}, f32[64]{0:T(128)}, u32[]{:S(2)}) copy-start(f32[64]{0:T(128)} %param.11) | copy-start | bytes 772
  567.7 2.9 copy-start.1
  573.6 3.0 copy-start.7
  576.6 0.6 copy-start.8
  581.8 2.9 copy-start.1
  587.7 3.0 copy-start.7
  590.7 0.6 copy-start.8
  595.9 2.9 copy-start.1
  601.8 3.0 copy-start.7
  604.8 0.6 copy-start.8
  610.0 2.9 copy-start.1
  615.9 3.0 copy-start.7
  618.9 0.6 copy-start.8
  624.2 2.9 copy-start.1
  630.0 3.0 copy-start.7
  633.1 0.6 copy-start.8
  638.3 2.9 copy-start.1
  644.1 3.0 copy-start.7
  647.2 0.6 copy-start.8
  652.4 2.9 copy-start.1
  658.2 3.0 copy-start.7
  661.3 0.6 copy-start.8
  666.5 2.9 copy-start.1
  672.4 3.0 copy-start.7
  675.4 0.6 copy-start.8
  680.6 2.9 copy-start.1
  686.5 3.0 copy-start.7
  689.5 0.6 copy-start.8
  694.7 2.9 copy-start.1
  700.6 3.0 copy-start.7
  703.6 0.6 copy-start.8
  708.8 2.9 copy-start.1
  714.7 3.0 copy-start.7
  717.7 0.6 copy-start.8
  723.0 2.9 copy-start.1
  728.8 3.0 copy-start.7
  731.8 0.6 copy-start.8
  732.4 55.7 %copy-start.2 = (f32[768,128]{1,0:T(8,128)}, f32[768,128]{1,0:T(8,128)S(1)}, u32[]{:S(2)}) copy-start(f32[768,128]{1,0:T(8,128)S(1)} %get-tuple-element.62) | copy-start | bytes 1179652
  733.4 122.7 %reduce-scatter.6.cloned.1.call-start = ((), (), s32[]{:S(2)}) async-start(), calls=%async_computation.4 | async-start | bytes 491520 | tf_op jit(solution)/shard_map/reduce_scatter | solution.py:48
  788.2 346.5 %all-reduce.6.cloned.1.call-start = ((), (), s32[]{:S(2)}) async-start(), calls=%async_computation.7 | async-start | bytes 9437184
Sparse Core Ops, SparseCore 0:
  12.3 254.7 all-gather.6
  268.8 294.1 all-gather.4
  733.5 87.6 reduce-scatter.7
  823.8 32.2 reduce-scatter.5
  861.5 273.0 all-reduce.5
